TPU v7x, 32 devices: a whole 2x2x4 slice. The times are simulated.
32 devices in a mesh: row: 4 (over y, x), col: 8 (over z, core).
Axes of the slice: x: 2, y: 2, z: 4, core: 2. Of those that a mesh axis runs over, the one named last changes fastest.
Arguments:
- targets: float32 [2, 16384], P(None, ('row', 'col')), may hold values from 0 to 1
- sources: bfloat16 [2, 16384], P(None, 'col'), may hold values from 0 to 1
- omega: bfloat16 [256, 16384], P(None, 'col'), may hold values from -0.046875 to 0.046875
- tree_order: int32 [16384], P(('row', 'col')), may hold values from 0 to 16383, each once
- leaf_pivots: int32 [32, 128], P(('row', 'col')), may hold values from 0 to 511, all different within a row
- pivots_one: int32 [16, 128], replicated, may hold values from 0 to 255, all different within a row
- pivots_two: int32 [8, 128], replicated, may hold values from 0 to 255, all different within a row
- pivots_three: int32 [4, 128], replicated, may hold values from 0 to 255, all different within a row
Outputs:
- leaf_interp: float32 [16384, 128], P(('row', 'col'))
- level_one_interp: float32 [4096, 128], P(('row', 'col'))
- level_two_interp: float32 [2048, 128], P(('row', 'col'))
- level_three_interp: float32 [1024, 128], P(('row', 'col'))
- root_sketch: float32 [512, 256], P(('row', 'col'))
Inputs may be any that keep to these rules, and one draw needn't show every extreme that they name: tree_order names every target point once. `leaf_pivots`: each row names 128 distinct positions. `pivots_one`: each row names 128 distinct positions. `pivots_two`: each row names 128 distinct positions. `pivots_three`: each row names 128 distinct positions.
All inputs are finite; a program needn't handle non-finite values.
Results may differ from a plain program's by a relative error of at most 0.0074.
Values may be sent and summed in bfloat16 or wider, within the bound.
A program may use at most 192 MiB of HBM per device.

v0:
```python
import math
import jax
import jax.numpy as jnp
from jax import lax
from jax.sharding import PartitionSpec as P

LEAF = 512
S = 256
LEVELS = 3
RIDGE = 0.1
DELTA_SQUARED = 0.0001


def partner_2(block, axis, stride):
    count = lax.axis_size(axis)
    route = []
    for low in range(count):
        high = low | 1 << stride
        if high != low and high < count:
            route += [(low, high), (high, low)]
    return lax.ppermute(block, axis, route)


def kernel_block(points, source_pts):
    delta_x = points[0][:, None] - source_pts[0][None, :].astype(jnp.float32)
    delta_y = points[1][:, None] - source_pts[1][None, :].astype(jnp.float32)
    return (-0.5 * jnp.log(delta_x * delta_x + delta_y * delta_y + DELTA_SQUARED)).astype(
        jnp.bfloat16
    )


def select_factor(candidates, pivots):
    chosen = jnp.take(candidates, pivots, axis=0)
    gram_matrix = jnp.dot(chosen, chosen.T, precision=lax.Precision.HIGHEST)
    ridge_shift = RIDGE * (jnp.trace(gram_matrix) / chosen.shape[0] + 1e-06)
    shifted = gram_matrix + ridge_shift * jnp.eye(chosen.shape[0], dtype=gram_matrix.dtype)
    return (chosen, jnp.linalg.cholesky(shifted))


def solve_rows(chosen, factor, row_block):
    right_side = jnp.dot(chosen, row_block.T, precision=lax.Precision.HIGHEST)
    first = lax.linalg.triangular_solve(factor, right_side, left_side=True, lower=True)
    second = lax.linalg.triangular_solve(
        factor, first, left_side=True, lower=True, transpose_a=True
    )
    return second.T


def sketch_product(points, source_pts, weights):
    panel = kernel_block(points, source_pts)
    return lax.dot_general(
        panel, weights, (((1,), (1,)), ((), ())), preferred_element_type=jnp.float32
    )


def body(targets, sources, omega, tree_order, leaf_pivots, pivots_one, pivots_two, pivots_three):
    everyone = lax.all_gather(targets, ("row", "col"), axis=1, tiled=True)
    col_count = lax.axis_size("col")
    col_index = lax.axis_index("col")
    row_index = lax.axis_index("row")
    global_index = row_index * col_count + col_index
    positions = lax.all_gather(tree_order, "col", axis=0, tiled=True)
    placed = jnp.take(everyone, positions, axis=1)
    block_len = math.gcd(LEAF * lax.axis_size("col"), LEAF)
    blocks = placed.reshape(2, LEAF * lax.axis_size("col") // block_len, block_len).transpose(
        1, 0, 2
    )

    def one_block(points):
        return sketch_product(points, sources, omega)

    leaf_sketch = lax.psum_scatter(
        lax.map(one_block, blocks).reshape(LEAF * lax.axis_size("col"), S),
        "col",
        scatter_dimension=0,
        tiled=True,
    )
    chosen, factor = select_factor(leaf_sketch, leaf_pivots[0])
    results = [solve_rows(chosen, factor, leaf_sketch)]
    tables = (pivots_one, pivots_two, pivots_three)
    for section in range(LEVELS):
        partner = partner_2(chosen, "col", section)
        high_half = col_index >> section & 1 == 1
        candidates = jnp.where(
            high_half, jnp.concatenate([partner, chosen], 0), jnp.concatenate([chosen, partner], 0)
        )
        node_index = global_index >> section + 1
        node_pivots = lax.dynamic_index_in_dim(tables[section], node_index, 0, keepdims=False)
        group_size = 2 ** (section + 1)
        share_rows = candidates.shape[0] // group_size
        my_rows = lax.dynamic_slice_in_dim(
            candidates, col_index % group_size * share_rows, share_rows, 0
        )
        chosen, factor = select_factor(candidates, node_pivots)
        results.append(solve_rows(chosen, factor, my_rows))
    root_rows = chosen.shape[0] // 2**LEVELS
    root_share = lax.dynamic_slice_in_dim(chosen, col_index % 2**LEVELS * root_rows, root_rows, 0)
    return (results[0], results[1], results[2], results[3], root_share)


def solution(mesh):
    return jax.shard_map(
        body,
        mesh=mesh,
        in_specs=(
            P(None, ("row", "col")),
            P(None, "col"),
            P(None, "col"),
            P(("row", "col")),
            P(("row", "col"), None),
            P(),
            P(),
            P(),
        ),
        out_specs=(
            P(("row", "col"), None),
            P(("row", "col"), None),
            P(("row", "col"), None),
            P(("row", "col"), None),
            P(("row", "col"), None),
        ),
        check_vma=False,
    )
```

profile of v0, /device:TPU:0, one launch (start us, length us, event | category | flops | bytes accessed | tf_op | source)
XLA Modules:
  0.0 331.0 jit_solution(13750035460715798089)
XLA Ops:
  7.2 14.6 %all-gather = s32[8,1,512]{2,1,0:T(1,128)S(1)} all-gather(s32[1,1,512]{2,1,0:T(1,128)} %bitcast.123), channel_id=1, replica_groups=mesh['row'=4,'col'=8] {'col'}, dimensions={0}, use_global_device_ids=true | all-gather | bytes 18432 | tf_op jit(solution)/shard_map/all_gather | solution.py:62
  22.7 103.6 %all_gather.7 = f32[2,16384]{0,1:T(8,128)} all-gather(f32[2,512]{0,1:T(8,128)S(1)} %copy.23), channel_id=1, replica_groups=mesh['row'=4,'col'=8] {'row','col'}, dimensions={1}, use_global_device_ids=true | all-gather | bytes 135168 | tf_op jit(solution)/shard_map/all_gather | solution.py:57
  126.3 14.1 %gather_fusion = f32[4096,2]{1,0:T(8,128)S(1)} fusion(f32[2,16384]{0,1:T(8,128)} %all_gather.7, s32[4096]{0:T(1024)S(1)} %fusion.51), kind=kCustom, calls=%fused_computation.3 | custom fusion | bytes 81920 | tf_op jit(solution)/shard_map/jit(_take)/gather | solution.py:63
  141.2 18.9 %while.10 = (s32[]{:T(128)}, f32[8,512,256]{2,1,0:T(8,128)}, f32[8,2,512]{2,1,0:T(2,128)S(1)}, bf16[2,2048]{1,0:T(2,128)(2,1)S(1)}, bf16[256,2048]{1,0:T(8,128)(2,1)S(1)}, /*index=5*/s32[]{:T(128)}, s32[]{:T(128)}, s32[]{}) while((s32[]{:T(128)}, f32[8,512,256]{2,1,0:T(8,128)}, f32[8,2,512]{2,1,0:T(2,128)S(1)}, bf16[2,2048]{1,0:T(2,128)(2,1)S(1)}, ...), condition=%wide.region_1.2_spmd, body=%wide.region_0.1_spmd.sunk | while | flops 545263616 | bytes 1626729 | solution.py:73
  141.2 2.4 fusion.85
  143.6 2.4 fusion.85
  146.0 2.3 fusion.85
  148.4 2.3 fusion.85
  150.7 2.3 fusion.85
  153.1 2.3 fusion.85
  155.4 2.3 fusion.85
  157.8 2.3 fusion.85
  162.4 48.2 %reduce-scatter.2.cloned.1.call-done = f32[512,256]{1,0:T(8,128)} async-done(((f32[4096,256]{1,0:T(8,128)}), f32[512,256]{1,0:T(8,128)}) %reduce-scatter.2.cloned.1.call-update) | async-done | bytes 524304 | tf_op jit(solution)/shard_map/reduce_scatter | solution.py:72
  210.6 1.8 gather_fusion.1
  214.3 11.7 %cholesky.74 = f32[128,128]{1,0:T(8,128)S(1)} custom-call(f32[128,128]{1,0:T(8,128)S(1)} %copy.26), custom_call_target="Cholesky" | custom-call | tf_op jit(solution)/shard_map/jit(cholesky)/cholesky | solution.py:37
  227.4 9.8 %custom-call.22 = f32[1,128,128]{1,2,0:T(8,128)S(1)} custom-call(f32[1,128,128]{2,1,0:T(8,128)S(1)} %fusion.7), custom_call_target="InvertDiagBlocksLowerTriangular" | custom-call | tf_op jit(solution)/shard_map/triangular_solve | solution.py:43
  237.2 1.7 fusion.59
  243.4 11.9 %cholesky.85 = f32[128,128]{1,0:T(8,128)S(1)} custom-call(f32[128,128]{1,0:T(8,128)S(1)} %copy.28), custom_call_target="Cholesky" | custom-call | tf_op jit(solution)/shard_map/jit(cholesky)/cholesky | solution.py:37
  256.6 9.8 %custom-call.23 = f32[1,128,128]{1,2,0:T(8,128)S(1)} custom-call(f32[1,128,128]{2,1,0:T(8,128)S(1)} %fusion.8), custom_call_target="InvertDiagBlocksLowerTriangular" | custom-call | tf_op jit(solution)/shard_map/triangular_solve | solution.py:43
  268.8 1.5 collective-permute-start.2
  272.0 11.7 %cholesky.96 = f32[128,128]{1,0:T(8,128)S(1)} custom-call(f32[128,128]{1,0:T(8,128)S(1)} %copy.30), custom_call_target="Cholesky" | custom-call | tf_op jit(solution)/shard_map/jit(cholesky)/cholesky | solution.py:37
  285.1 9.8 %custom-call.24 = f32[1,128,128]{1,2,0:T(8,128)S(1)} custom-call(f32[1,128,128]{2,1,0:T(8,128)S(1)} %fusion.9), custom_call_target="InvertDiagBlocksLowerTriangular" | custom-call | tf_op jit(solution)/shard_map/triangular_solve | solution.py:43
  299.0 12.0 %cholesky.107 = f32[128,128]{1,0:T(8,128)S(1)} custom-call(f32[128,128]{1,0:T(8,128)S(1)} %copy.32), custom_call_target="Cholesky" | custom-call | tf_op jit(solution)/shard_map/jit(cholesky)/cholesky | solution.py:37
  312.3 9.8 %custom-call.25 = f32[1,128,128]{1,2,0:T(8,128)S(1)} custom-call(f32[1,128,128]{2,1,0:T(8,128)S(1)} %fusion.10), custom_call_target="InvertDiagBlocksLowerTriangular" | custom-call | tf_op jit(solution)/shard_map/triangular_solve | solution.py:43
  (99 shorter events, 23.1 us)
Async XLA Ops:
  7.2 203.4 %reduce-scatter.2.cloned.1.call-start = ((), (), s32[]{:S(2)}) async-start(), calls=%async_computation.1 | async-start | bytes 4718592 | tf_op jit(solution)/shard_map/reduce_scatter | solution.py:72
  22.7 118.5 %copy-start = (bf16[2,2048]{1,0:T(2,128)(2,1)S(1)}, bf16[2,2048]{1,0:T(2,128)(2,1)}, u32[]{:S(2)}) copy-start(bf16[2,2048]{1,0:T(2,128)(2,1)} %param.14) | copy-start | bytes 24580
  22.7 118.5 %copy-start.1 = (bf16[256,2048]{1,0:T(8,128)(2,1)S(1)}, bf16[256,2048]{1,0:T(8,128)(2,1)}, u32[]{:S(2)}) copy-start(bf16[256,2048]{1,0:T(8,128)(2,1)} %param.15) | copy-start | bytes 3145732
  160.1 2.2 copy-start.2
  212.5 28.1 %collective-permute-start = (f32[128,256]{1,0:T(8,128)S(1)}, f32[128,256]{1,0:T(8,128)S(1)}, u32[]{:S(2)}, u32[]{:S(2)}) collective-permute-start(f32[128,256]{1,0:T(8,128)S(1)} %broadcast_select_fusion.3), channel_id=1, source_target_pairs={{0,1},{1,0},{2,3},{3,2},{4,5},{5,4},{6,7},{7,6},{8,9},{9,8},{10,11... | collective-permute-start | bytes 393224 | tf_op jit(solution)/shard_map/ppermute | solution.py:21
  241.5 26.4 %collective-permute-start.1 = (f32[128,256]{1,0:T(8,128)S(1)}, f32[128,256]{1,0:T(8,128)S(1)}, u32[]{:S(2)}, u32[]{:S(2)}) collective-permute-start(f32[128,256]{1,0:T(8,128)S(1)} %broadcast_select_fusion.2), channel_id=1, source_target_pairs={{0,2},{2,0},{1,3},{3,1},{4,6},{6,4},{5,7},{7,5},{8,10},{10,8},{9,1... | collective-permute-start | bytes 393224 | tf_op jit(solution)/shard_map/ppermute | solution.py:21
  268.8 27.6 %collective-permute-start.2 = (f32[128,256]{1,0:T(8,128)S(1)}, f32[128,256]{1,0:T(8,128)S(1)}, u32[]{:S(2)}, u32[]{:S(2)}) collective-permute-start(f32[128,256]{1,0:T(8,128)S(1)} %broadcast_select_fusion.1), channel_id=1, source_target_pairs={{0,4},{4,0},{1,5},{5,1},{2,6},{6,2},{3,7},{7,3},{8,12},{12,8},{9,1... | collective-permute-start | bytes 393224 | tf_op jit(solution)/shard_map/ppermute | solution.py:21
Sparse Core Ops, SparseCore 0:
  160.3 50.2 reduce-scatter.1
where the time goes:
time: 331 us
  blocking collectives  118 us (36%)
  other arithmetic  94.6 us (29%)
  waiting for transfers between devices  48.2 us (15%)
  matrix products  29.9 us (9%)
  local copies, waits for them, and re-layouts  21.1 us (6%)
  between operations  17.1 us (5%)
    all_gather x1, blocking collectives, body(): everyone = lax.all_gather(targets, ('row', 'col'), axis=1, tiled=True)  104 us
    another operation x12, other arithmetic, select_factor(): return (chosen, jnp.linalg.cholesky(shifted))  50 us
    reduce_scatter x1, waiting for transfers between devices, body(): lax.psum_scatter(lax.map(one_block, blocks).reshape(LEAF * lax.axis_size(...  48.2 us
    another operation x8, other arithmetic, solve_rows(): lax.linalg.triangular_solve(factor, first, left_side=True, lower=True, tr...  41.9 us
    dot_general x8, matrix products, sketch_product(): lax.dot_general(panel, weights, (((1,), (1,)), ((), ())), preferred_eleme...  18.7 us
    gather x2, local copies, waits for them, and re-layouts, body(): placed = jnp.take(everyone, positions, axis=1)  14.8 us
    all_gather x1, blocking collectives, body(): positions = lax.all_gather(tree_order, 'col', axis=0, tiled=True)  14.6 us
  transfers between devices with their start and end apart: 4, of which 1 were waited for; matrix products, arithmetic and copies ran while one was open for 24% of the time, Pallas kernels for 0%

commit v1 on v0

--- a/solution.py
+++ b/solution.py
@@ -54,7 +54,8 @@
 
 
 def body(targets, sources, omega, tree_order, leaf_pivots, pivots_one, pivots_two, pivots_three):
-    everyone = lax.all_gather(targets, ("row", "col"), axis=1, tiled=True)
+    pieces = lax.all_gather(targets, ("row", "col"))
+    everyone = jnp.concatenate(pieces, axis=1)
     col_count = lax.axis_size("col")
     col_index = lax.axis_index("col")
     row_index = lax.axis_index("row")

time: 331 us -> 269 us (0.81)
  blocking collectives: 118 us -> 55.6 us
  waiting for transfers between devices: 48.2 us -> 44.1 us
  local copies, waits for them, and re-layouts: 21.1 us -> 25.1 us
    all_gather x1, blocking collectives: 104 us -> 41 us  [body(): pieces = lax.all_gather(targets, ('row', 'col'))]
    reshape x0 -> x1, local copies, waits for them, and re-layouts: none -> 4.82 us  [body(): everyone = jnp.concatenate(pieces, axis=1)]
    reduce_scatter x1, waiting for transfers between devices: 48.2 us -> 44.1 us  [body(): lax.psum_scatter(lax.map(one_block, blocks).reshape(LEAF * lax.axis_size(...]
  transfers between devices with their start and end apart: 4 -> 4, of which waited for: 1 -> 1; matrix products, arithmetic and copies ran while one was open for 24% -> 30% of each run, Pallas kernels for 0% -> 0%
where the time goes in v1:
time: 269 us; the launch traced here: 268 us
  other arithmetic  94.7 us (35%)
  blocking collectives  55.6 us (21%)
  waiting for transfers between devices  44.1 us (16%)
  matrix products  29.9 us (11%)
  local copies, waits for them, and re-layouts  25.1 us (9%)
  between operations  17.1 us (6%)
    another operation x12, other arithmetic, select_factor(): return (chosen, jnp.linalg.cholesky(shifted))  50 us
    reduce_scatter x1, waiting for transfers between devices, body(): lax.psum_scatter(lax.map(one_block, blocks).reshape(LEAF * lax.axis_size(...  44.1 us
    another operation x8, other arithmetic, solve_rows(): lax.linalg.triangular_solve(factor, first, left_side=True, lower=True, tr...  41.9 us
    all_gather x1, blocking collectives, body(): pieces = lax.all_gather(targets, ('row', 'col'))  41 us
    dot_general x8, matrix products, sketch_product(): lax.dot_general(panel, weights, (((1,), (1,)), ((), ())), preferred_eleme...  18.7 us
    gather x2, local copies, waits for them, and re-layouts, body(): placed = jnp.take(everyone, positions, axis=1)  14.8 us
    all_gather x1, blocking collectives, body(): positions = lax.all_gather(tree_order, 'col', axis=0, tiled=True)  14.6 us
  transfers between devices with their start and end apart: 4, of which 1 were waited for; matrix products, arithmetic and copies ran while one was open for 30% of the time, Pallas kernels for 0%

profile of v1, /device:TPU:0, one launch (start us, length us, event | category | flops | bytes accessed | tf_op | source)
XLA Modules:
  0.0 268.3 jit_solution(9994639898182698676)
XLA Ops:
  7.2 14.6 %all-gather.1 = s32[8,1,512]{2,1,0:T(1,128)S(1)} all-gather(s32[1,1,512]{2,1,0:T(1,128)} %bitcast.129), channel_id=1, replica_groups=mesh['row'=4,'col'=8] {'col'}, dimensions={0}, use_global_device_ids=true | all-gather | bytes 18432 | tf_op jit(solution)/shard_map/all_gather | solution.py:63
  21.9 41.0 %all-gather.2 = f32[32,2,512]{2,1,0:T(2,128)S(1)} all-gather(f32[1,2,512]{2,1,0:T(2,128)} %bitcast.128), channel_id=2, replica_groups=mesh['row'=4,'col'=8] {'row','col'}, dimensions={0}, use_global_device_ids=true | all-gather | bytes 135168 | tf_op jit(solution)/shard_map/all_gather | solution.py:57
  62.9 4.8 %copy.23 = f32[2,32,512]{0,2,1:T(8,128)} copy(f32[2,32,512]{2,0,1:T(2,128)S(1)} %bitcast.121) | data formatting | bytes 262144 | tf_op jit(solution)/shard_map/reshape | solution.py:58
  67.7 14.1 %gather_fusion = f32[4096,2]{1,0:T(8,128)S(1)} fusion(f32[2,16384]{0,1:T(8,128)} %bitcast.118, s32[4096]{0:T(1024)S(1)} %fusion.51), kind=kCustom, calls=%fused_computation.3 | custom fusion | bytes 81920 | tf_op jit(solution)/shard_map/jit(_take)/gather | solution.py:64
  82.5 18.9 %while.10 = (s32[]{:T(128)}, f32[8,512,256]{2,1,0:T(8,128)}, f32[8,2,512]{2,1,0:T(2,128)S(1)}, bf16[2,2048]{1,0:T(2,128)(2,1)S(1)}, bf16[256,2048]{1,0:T(8,128)(2,1)S(1)}, /*index=5*/s32[]{:T(128)}, s32[]{:T(128)}, s32[]{}) while((s32[]{:T(128)}, f32[8,512,256]{2,1,0:T(8,128)}, f32[8,2,512]{2,1,0:T(2,128)S(1)}, bf16[2,2048]{1,0:T(2,128)(2,1)S(1)}, ...), condition=%wide.region_1.2_spmd, body=%wide.region_0.1_spmd.sunk | while | flops 545263616 | bytes 1626729 | solution.py:74
  82.6 2.4 fusion.85
  85.0 2.4 fusion.85
  87.4 2.3 fusion.85
  89.7 2.3 fusion.85
  92.1 2.3 fusion.85
  94.5 2.3 fusion.85
  96.8 2.3 fusion.85
  99.1 2.3 fusion.85
  103.7 44.1 %reduce-scatter.2.cloned.1.call-done = f32[512,256]{1,0:T(8,128)} async-done(((f32[4096,256]{1,0:T(8,128)}), f32[512,256]{1,0:T(8,128)}) %reduce-scatter.2.cloned.1.call-update) | async-done | bytes 524304 | tf_op jit(solution)/shard_map/reduce_scatter | solution.py:73
  147.8 1.8 gather_fusion.1
  151.6 11.7 %cholesky.74 = f32[128,128]{1,0:T(8,128)S(1)} custom-call(f32[128,128]{1,0:T(8,128)S(1)} %copy.26), custom_call_target="Cholesky" | custom-call | tf_op jit(solution)/shard_map/jit(cholesky)/cholesky | solution.py:37
  164.6 9.8 %custom-call.22 = f32[1,128,128]{1,2,0:T(8,128)S(1)} custom-call(f32[1,128,128]{2,1,0:T(8,128)S(1)} %fusion.7), custom_call_target="InvertDiagBlocksLowerTriangular" | custom-call | tf_op jit(solution)/shard_map/triangular_solve | solution.py:43
  174.5 1.7 fusion.59
  180.7 11.9 %cholesky.85 = f32[128,128]{1,0:T(8,128)S(1)} custom-call(f32[128,128]{1,0:T(8,128)S(1)} %copy.28), custom_call_target="Cholesky" | custom-call | tf_op jit(solution)/shard_map/jit(cholesky)/cholesky | solution.py:37
  193.9 9.8 %custom-call.23 = f32[1,128,128]{1,2,0:T(8,128)S(1)} custom-call(f32[1,128,128]{2,1,0:T(8,128)S(1)} %fusion.8), custom_call_target="InvertDiagBlocksLowerTriangular" | custom-call | tf_op jit(solution)/shard_map/triangular_solve | solution.py:43
  209.3 11.7 %cholesky.96 = f32[128,128]{1,0:T(8,128)S(1)} custom-call(f32[128,128]{1,0:T(8,128)S(1)} %copy.30), custom_call_target="Cholesky" | custom-call | tf_op jit(solution)/shard_map/jit(cholesky)/cholesky | solution.py:37
  222.3 9.8 %custom-call.24 = f32[1,128,128]{1,2,0:T(8,128)S(1)} custom-call(f32[1,128,128]{2,1,0:T(8,128)S(1)} %fusion.9), custom_call_target="InvertDiagBlocksLowerTriangular" | custom-call | tf_op jit(solution)/shard_map/triangular_solve | solution.py:43
  236.3 12.0 %cholesky.107 = f32[128,128]{1,0:T(8,128)S(1)} custom-call(f32[128,128]{1,0:T(8,128)S(1)} %copy.32), custom_call_target="Cholesky" | custom-call | tf_op jit(solution)/shard_map/jit(cholesky)/cholesky | solution.py:37
  249.6 9.8 %custom-call.25 = f32[1,128,128]{1,2,0:T(8,128)S(1)} custom-call(f32[1,128,128]{2,1,0:T(8,128)S(1)} %fusion.10), custom_call_target="InvertDiagBlocksLowerTriangular" | custom-call | tf_op jit(solution)/shard_map/triangular_solve | solution.py:43
  (99 shorter events, 23.7 us)
Async XLA Ops:
  7.2 140.7 %reduce-scatter.2.cloned.1.call-start = ((), (), s32[]{:S(2)}) async-start(), calls=%async_computation.1 | async-start | bytes 4718592 | tf_op jit(solution)/shard_map/reduce_scatter | solution.py:73
  62.9 19.7 %copy-start = (bf16[2,2048]{1,0:T(2,128)(2,1)S(1)}, bf16[2,2048]{1,0:T(2,128)(2,1)}, u32[]{:S(2)}) copy-start(bf16[2,2048]{1,0:T(2,128)(2,1)} %param.14) | copy-start | bytes 24580
  62.9 19.7 %copy-start.1 = (bf16[256,2048]{1,0:T(8,128)(2,1)S(1)}, bf16[256,2048]{1,0:T(8,128)(2,1)}, u32[]{:S(2)}) copy-start(bf16[256,2048]{1,0:T(8,128)(2,1)} %param.15) | copy-start | bytes 3145732
  101.5 2.2 copy-start.2
  149.7 28.1 %collective-permute-start = (f32[128,256]{1,0:T(8,128)S(1)}, f32[128,256]{1,0:T(8,128)S(1)}, u32[]{:S(2)}, u32[]{:S(2)}) collective-permute-start(f32[128,256]{1,0:T(8,128)S(1)} %broadcast_select_fusion.3), channel_id=1, source_target_pairs={{0,1},{1,0},{2,3},{3,2},{4,5},{5,4},{6,7},{7,6},{8,9},{9,8},{10,11... | collective-permute-start | bytes 393224 | tf_op jit(solution)/shard_map/ppermute | solution.py:21
  178.7 26.4 %collective-permute-start.1 = (f32[128,256]{1,0:T(8,128)S(1)}, f32[128,256]{1,0:T(8,128)S(1)}, u32[]{:S(2)}, u32[]{:S(2)}) collective-permute-start(f32[128,256]{1,0:T(8,128)S(1)} %broadcast_select_fusion.2), channel_id=1, source_target_pairs={{0,2},{2,0},{1,3},{3,1},{4,6},{6,4},{5,7},{7,5},{8,10},{10,8},{9,1... | collective-permute-start | bytes 393224 | tf_op jit(solution)/shard_map/ppermute | solution.py:21
  206.1 27.6 %collective-permute-start.2 = (f32[128,256]{1,0:T(8,128)S(1)}, f32[128,256]{1,0:T(8,128)S(1)}, u32[]{:S(2)}, u32[]{:S(2)}) collective-permute-start(f32[128,256]{1,0:T(8,128)S(1)} %broadcast_select_fusion.1), channel_id=1, source_target_pairs={{0,4},{4,0},{1,5},{5,1},{2,6},{6,2},{3,7},{7,3},{8,12},{12,8},{9,1... | collective-permute-start | bytes 393224 | tf_op jit(solution)/shard_map/ppermute | solution.py:21
Sparse Core Ops, SparseCore 0:
  101.6 46.1 reduce-scatter.1
